TPU v7x, 512 devices: a whole 4x8x8 slice. The times are simulated.
512 devices in a mesh: sect: 4 (over z_lo, core), blk: 128 (over z_hi, x, y).
Axes of the slice: x: 4, y: 8, z: 8 (z_hi: 4, z_lo: 2; z = z_hi * 2 + z_lo), core: 2. Of those that a mesh axis runs over, the one named last changes fastest.
Arguments:
- last_perceptron_activations: bfloat16 [512, 192, 4304], P(('sect', 'blk')), may hold values from -6 to 6
- caption_reduction_matrix: bfloat16 [4304, 1152], P(None, 'blk'), may hold values from -0.09375 to 0.09375
- picture_reduction_matrix: bfloat16 [4304, 1152], P(None, 'blk'), may hold values from -0.09375 to 0.09375
- caption_offset_vector: float32 [1152], replicated, may hold values from -0.6 to 0.6
- picture_offset_vector: float32 [1152], replicated, may hold values from -0.6 to 0.6
- score_multiplier_array: float32 [1], replicated, may hold values from 4 to 16
- match_score_offset: float32 [1], replicated, may hold values from -6 to -2
- caption_match_position: int32 [384], replicated, may hold values from 0 to 383, each once
Outputs:
- text_grad: float32 [384, 4304], P('blk', 'sect')
Inputs may be any that keep to these rules, and one draw needn't show every extreme that they name: `caption_match_position`: each text index appears exactly once, so every image has exactly one paired text.
All inputs are finite; a program needn't handle non-finite values.
Results may differ from a plain program's by a relative error of at most 0.013.
Values may be sent and summed in bfloat16 or wider, within the bound.
A program may use at most 128 MiB of HBM per device.

v0:
```python
import jax
import jax.numpy as jnp
from jax import lax
from jax.sharding import Mesh
from jax.sharding import PartitionSpec as P

D = 1152
FF = 4304
TXT_LEN = 64
IMG_TOK = 192
BLK = ("blk_0", "blk_1", "blk_2")
SECT_BLK = ("sect", "blk_0", "blk_1", "blk_2")


def broadcast(x, axis, root):
    return lax.dynamic_index_in_dim(lax.all_gather(x, axis), root, 0, keepdims=False)


def joined_along(parts, dim):
    lengths = list(parts.shape[1:])
    lengths[dim] *= parts.shape[0]
    return jnp.moveaxis(parts, 0, dim).reshape(lengths)


def gather_in_order(x, axes, sequence):
    parts = x[None]
    for k in sequence:
        parts = lax.all_gather(parts, axes[k], axis=0, tiled=True)
    held = [lax.axis_size(axes[k]) for k in reversed(sequence)]
    parts = parts.reshape(*held, *x.shape)
    turned = sorted(range(len(sequence)), key=lambda place: sequence[len(sequence) - 1 - place])
    return parts.transpose(*turned, *range(len(sequence), parts.ndim)).reshape(-1, *x.shape)


def gathered_by_axis(x, axes, sequence, dim):
    return joined_along(gather_in_order(x, axes, sequence), dim)


def reduced_to_own(parts, axes, sequence):
    inside = parts.shape[1:]
    parts = parts.reshape(*(lax.axis_size(a) for a in axes), *inside)
    parts = jnp.moveaxis(parts, sequence, range(len(axes))).reshape(-1, *inside)
    for k in sequence:
        parts = lax.psum_scatter(parts, axes[k], scatter_dimension=0, tiled=True)
    return parts[0]


def cut_along(x, dim, count):
    before, after = (x.shape[:dim], x.shape[dim + 1 :])
    return jnp.moveaxis(x.reshape(*before, count, -1, *after), dim, 0)


def summed_rows(x, axes, sequence, dim):
    count = lax.axis_size(axes)
    return reduced_to_own(cut_along(x, dim, count), axes, sequence)


def copy_for_each(x, axis):
    count = lax.axis_size(axis)
    return lax.all_to_all(jnp.broadcast_to(x[None], (count, *x.shape)), axis, 0, 0, tiled=True)


def of_everyone(x, axis):
    return copy_for_each(x, axis).sum(axis=0)


def unit_rows(pool):
    inv = lax.rsqrt(jnp.sum(pool * pool, axis=-1, keepdims=True) + 1e-06)
    return (pool * inv, inv)


def on_device(
    last_perceptron_activations,
    caption_reduction_matrix,
    picture_reduction_matrix,
    caption_offset_vector,
    picture_offset_vector,
    score_multiplier_array,
    match_score_offset,
    caption_match_position,
):
    hidden = last_perceptron_activations[0]
    sect_index = lax.axis_index("sect")
    blk_index = lax.axis_index(BLK)
    blk_count = lax.axis_size(BLK)
    sect_count = lax.axis_size("sect")
    rows = hidden.shape[0]
    txt_count = rows // TXT_LEN
    img_count = rows // IMG_TOK
    width = FF // sect_count
    is_text = sect_index == 0
    live = jnp.where(is_text, 0.0, 1.0).astype(jnp.float32)
    w_local = jnp.where(is_text, caption_reduction_matrix, picture_reduction_matrix)
    outs = jnp.dot(
        hidden, lax.all_gather(w_local, BLK, axis=1, tiled=True), preferred_element_type=jnp.float32
    )
    text_pool = jnp.mean(outs.reshape(txt_count, TXT_LEN, D), axis=1) + caption_offset_vector
    image_pool = jnp.mean(outs.reshape(img_count, IMG_TOK, D), axis=1) + picture_offset_vector
    text_pool = broadcast(text_pool, "sect", 0)
    text_unit, text_inv = unit_rows(text_pool)
    image_unit, image_inv = unit_rows(image_pool)
    text_emb = text_unit.astype(jnp.bfloat16)
    image_emb = image_unit.astype(jnp.bfloat16)
    similarity_multiplier = score_multiplier_array[0]
    shift_bias = match_score_offset[0]
    first = jnp.maximum((sect_index - 1) * blk_count + blk_index, 0) * img_count
    mine = lax.dynamic_slice_in_dim(caption_match_position, first, img_count)
    all_texts = gathered_by_axis(text_emb, BLK, (0, 1, 2), 0)
    count = all_texts.shape[0]
    logits = (
        similarity_multiplier
        * lax.dot_general(
            image_emb, all_texts, (((1,), (1,)), ((), ())), preferred_element_type=jnp.float32
        )
        + shift_bias
    )
    index_row = jnp.arange(count, dtype=jnp.int32)
    label = jnp.where(mine[:, None] == index_row[None, :], 1.0, -1.0).astype(jnp.float32)
    coef = (-label * jax.nn.sigmoid(-label * logits) * live).astype(jnp.bfloat16)
    acc_full = lax.dot_general(
        coef, image_emb, (((0,), (0,)), ((), ())), preferred_element_type=jnp.float32
    )
    acc = summed_rows(acc_full, BLK, (1, 2, 0), 0)
    acc = of_everyone(acc, "sect")
    grad = similarity_multiplier * acc
    grad_pool = (grad - text_unit * jnp.sum(text_unit * grad, axis=-1, keepdims=True)) * text_inv
    dy = grad_pool.astype(jnp.bfloat16)
    w_rows = lax.dynamic_slice_in_dim(caption_reduction_matrix, sect_index * width, width, 0)
    return lax.dot_general(
        dy,
        gathered_by_axis(w_rows, BLK, (0, 1, 2), 1),
        (((1,), (1,)), ((), ())),
        preferred_element_type=jnp.float32,
    )


def solution(mesh):
    finer = Mesh(
        mesh.devices.reshape(mesh.shape["sect"], 4, 4, 8), ("sect", "blk_0", "blk_1", "blk_2")
    )
    placed = (P(SECT_BLK, None, None), P(None, BLK), P(None, BLK), P(), P(), P(), P(), P())
    return jax.shard_map(
        on_device, mesh=finer, in_specs=placed, out_specs=P(BLK, "sect"), check_vma=False
    )
```

profile of v0, /device:TPU:2, one launch (start us, length us, event | category | flops | bytes accessed | tf_op | source)
XLA Modules:
  0.0 512.0 jit_solution(2313802400999751418)
XLA Ops:
  6.5 0.0 copy-start
  6.5 0.0 all-gather.8.cloned.1.call-start
  6.5 1.7 select_bitcast_fusion
  8.2 0.0 all-gather.8.cloned.1.call-update
  8.3 0.0 reduce-scatter.4.cloned.1.call-start
  9.6 1.3 dynamic_slice.10
  10.9 225.3 %all-gather.8.cloned.1.call-done = bf16[128,9,4304]{2,1,0:T(8,128)(2,1)} async-done(((bf16[1,9,4304]{2,1,0:T(8,128)(2,1)}), bf16[128,9,4304]{2,1,0:T(8,128)(2,1)}) %all-gather.8.cloned.1.call-update) | async-done | bytes 9916432 | tf_op jit(solution)/shard_map/all_gather | solution.py:95
  236.2 17.9 %reshape.152 = bf16[1152,4304]{1,0:T(8,128)(2,1)} reshape(bf16[128,9,4304]{2,1,0:T(8,128)(2,1)} %all-gather.8.cloned.1.call-done) | data formatting | bytes 19832832
  254.1 0.0 copy-done
  254.1 0.0 copy-start.2
  254.1 7.3 %fusion.14 = (f32[1152]{0:T(1024)S(1)}, f32[1152,192]{0,1:T(8,128)S(1)}) fusion(bf16[1152,4304]{1,0:T(8,128)(2,1)} %reshape.152, bf16[1,192,4304]{2,1,0:T(8,128)(2,1)S(1)} %copy-done), kind=kOutput, calls=%fused_computation.32 | convolution fusion | flops 1904171904 | bytes 12458496 | tf_op jit(solution)/shard_map/dot_general | solution.py:94
  261.4 0.1 reduce_sum.56
  261.4 0.0 copy-done.2
  261.5 5.3 %all_gather.26 = f32[4,3,1152]{2,1,0:T(4,128)S(1)} all-gather(f32[1,3,1152]{2,1,0:T(4,128)S(1)} %bitcast_add_fusion), channel_id=1, replica_groups=mesh['sect'=4,'blk_0'=4,'blk_1'=4,'blk_2'=8] {'sect'}, dimensions={0}, use_global_device_ids=true | all-gather | bytes 69120 | tf_op jit(solution)/shard_map/all_gather | solution.py:16
  266.7 0.1 fusion.4
  266.9 0.1 multiply_convert_fusion
  266.9 13.7 %all_gather.27 = bf16[4,3,1152]{2,1,0:T(4,128)(2,1)S(1)} all-gather(bf16[1,3,1152]{2,1,0:T(4,128)(2,1)S(1)} %multiply_convert_fusion), channel_id=1, replica_groups=mesh['sect'=4,'blk_0'=4,'blk_1'=4,'blk_2'=8] {'blk_0'}, dimensions={0}, use_global_device_ids=true | all-gather | bytes 34560 | tf_op jit(solution)/shard_map/all_gather | solution.py:28
  280.7 12.1 %all_gather.28 = bf16[16,3,1152]{2,1,0:T(4,128)(2,1)S(1)} all-gather(bf16[4,3,1152]{2,1,0:T(4,128)(2,1)S(1)} %all_gather.27), channel_id=1, replica_groups=mesh['sect'=4,'blk_0'=4,'blk_1'=4,'blk_2'=8] {'blk_1'}, dimensions={0}, use_global_device_ids=true | all-gather | bytes 138240 | tf_op jit(solution)/shard_map/all_gather | solution.py:28
  292.8 26.3 %all_gather.29 = bf16[128,3,1152]{2,0,1:T(8,128)(2,1)S(1)} all-gather(bf16[16,3,1152]{2,0,1:T(8,128)(2,1)S(1)} %copy.34), channel_id=1, replica_groups=mesh['sect'=4,'blk_0'=4,'blk_1'=4,'blk_2'=8] {'blk_2'}, dimensions={0}, use_global_device_ids=true | all-gather | bytes 995328 | tf_op jit(solution)/shard_map/all_gather | solution.py:28
  319.1 0.0 copy-start.1
  319.1 1.1 reshape.143
  320.3 1.9 copy.35
  322.2 1.5 reshape_reshape.4
  323.7 0.0 copy-done.1
  323.7 0.6 multiply_reduce_fusion
  325.1 1.5 convolution_reduce_fusion
  326.6 0.6 fusion.12
  327.2 0.2 reshape.149
  327.5 0.9 copy.36
  328.4 1.1 multiply_bitcast_fusion
  329.5 1.8 reshape.145
  331.3 0.0 reduce-scatter.4.cloned.1.call-update
  331.3 0.0 all-reduce.4.cloned.1.call-start
  331.4 26.4 %reduce-scatter.4.cloned.1.call-done = f32[32,3,1152]{2,0,1:T(8,128)} async-done(((f32[128,3,1152]{2,0,1:T(8,128)}), f32[32,3,1152]{2,0,1:T(8,128)}) %reduce-scatter.4.cloned.1.call-update) | async-done | bytes 442384 | tf_op jit(solution)/shard_map/reduce_scatter | solution.py:44
  357.8 0.0 all-reduce.4.cloned.1.call-update
  357.8 0.0 all-gather.6.cloned.1.call-start
  357.9 0.9 dynamic-slice_bitcast_fusion
  358.7 16.7 %all-gather.2 = bf16[4,1076,9]{1,2,0:T(8,128)(2,1)S(1)} all-gather(bf16[1,1076,9]{1,2,0:T(8,128)(2,1)S(1)} %dynamic-slice_bitcast_fusion), channel_id=2, replica_groups=mesh['sect'=4,'blk_0'=4,'blk_1'=4,'blk_2'=8] {'blk_0'}, dimensions={0}, use_global_device_ids=true | all-gather | bytes 96840 | tf_op jit(solution)/shard_map/all_gather | solution.py:28
  375.4 13.0 %all_gather.31 = bf16[16,1076,9]{1,2,0:T(8,128)(2,1)S(1)} all-gather(bf16[4,1076,9]{1,2,0:T(8,128)(2,1)S(1)} %all-gather.2), channel_id=1, replica_groups=mesh['sect'=4,'blk_0'=4,'blk_1'=4,'blk_2'=8] {'blk_1'}, dimensions={0}, use_global_device_ids=true | all-gather | bytes 387360 | tf_op jit(solution)/shard_map/all_gather | solution.py:28
  388.5 0.8 copy.38
  389.3 0.0 all-gather.6.cloned.1.call-update
  389.3 1.3 dynamic-slice
  390.6 1.2 dynamic-slice.2
  392.4 47.4 %all-reduce.4.cloned.1.call-done = f32[32,3,1152]{2,0,1:T(8,128)} async-done(((f32[32,3,1152]{2,0,1:T(8,128)}), f32[32,3,1152]{2,0,1:T(8,128)}) %all-reduce.4.cloned.1.call-update) | async-done | bytes 442384
  439.9 0.9 constant_dynamic-slice_fusion.1
  440.8 21.6 %all-reduce.1 = f32[4,3,1152]{2,0,1:T(4,128)S(1)} all-reduce(f32[4,3,1152]{2,0,1:T(4,128)S(1)} %constant_dynamic-slice_fusion.1), channel_id=5, replica_groups=mesh['sect'=4,'blk_0'=4,'blk_1'=4,'blk_2'=8] {'blk_0'}, use_global_device_ids=true, to_apply=%region_6.7.clone | all-reduce | flops 13824 | bytes 110592
  462.4 0.6 constant_dynamic-slice_fusion
  463.0 0.6 broadcast_in_dim.29
  463.6 3.3 all-to-all-start
  466.9 18.4 %all-gather.6.cloned.1.call-done = bf16[128,1076,9]{1,0,2:T(8,128)(2,1)} async-done(((bf16[16,1076,9]{1,0,2:T(8,128)(2,1)}), bf16[128,1076,9]{1,0,2:T(8,128)(2,1)}) %all-gather.6.cloned.1.call-update) | async-done | bytes 2479120 | tf_op jit(solution)/shard_map/all_gather | solution.py:28
  485.3 5.6 %reshape.146 = bf16[8,4,4,1076,9]{3,2,1,0,4:T(4,128)(2,1)} reshape(bf16[128,1076,9]{1,0,2:T(8,128)(2,1)} %all-gather.6.cloned.1.call-done) | data formatting | bytes 4958208 | tf_op jit(solution)/shard_map/reshape | solution.py:30
  490.9 5.6 %copy.41 = bf16[4,4,8,1076,9]{3,4,2,1,0:T(8,128)(2,1)} copy(bf16[4,4,8,1076,9]{3,0,1,2,4:T(4,128)(2,1)} %bitcast.69) | data formatting | bytes 4958208 | tf_op jit(solution)/shard_map/transpose | solution.py:22
  496.5 5.9 %reshape.148 = bf16[1076,1152]{0,1:T(8,128)(2,1)} reshape(bf16[1076,128,9]{0,2,1:T(8,128)(2,1)} %bitcast.68) | data formatting | bytes 4958208 | tf_op jit(solution)/shard_map/reshape | solution.py:22
  502.4 0.0 all-to-all-done
  502.5 0.2 fusion.6
  502.6 2.9 fusion.7
  (7 shorter events, 0.1 us)
Async XLA Ops:
  6.5 247.6 %copy-start = (bf16[1,192,4304]{2,1,0:T(8,128)(2,1)S(1)}, bf16[1,192,4304]{2,1,0:T(8,128)(2,1)}, u32[]{:S(2)}) copy-start(bf16[1,192,4304]{2,1,0:T(8,128)(2,1)} %param.8) | copy-start | bytes 4958212
  6.5 229.7 %all-gather.8.cloned.1.call-start = ((), (), s32[]{:S(2)}) async-start(), calls=%async_computation.4 | async-start | bytes 17965056 | tf_op jit(solution)/shard_map/all_gather | solution.py:95
  8.3 349.5 %reduce-scatter.4.cloned.1.call-start = ((), (), s32[]{:S(2)}) async-start(), calls=%async_computation.2 | async-start | bytes 2211840 | tf_op jit(solution)/shard_map/reduce_scatter | solution.py:44
  254.1 7.3 %copy-start.2 = (f32[1152]{0:T(1024)S(1)}, f32[1152]{0:T(1024)}, u32[]{:S(2)}) copy-start(f32[1152]{0:T(1024)} %param.11) | copy-start | bytes 13828
  319.1 4.6 copy-start.1
  331.3 108.5 %all-reduce.4.cloned.1.call-start = ((), (), s32[]{:S(2)}) async-start(), calls=%async_computation.5 | async-start | bytes 884736
  357.8 127.5 %all-gather.6.cloned.1.call-start = ((), (), s32[]{:S(2)}) async-start(), calls=%async_computation.3 | async-start | bytes 2985984 | tf_op jit(solution)/shard_map/all_gather | solution.py:28
  463.6 38.8 %all-to-all-start = ((f32[4,3,1152]{2,1,0:T(4,128)}), f32[4,3,1152]{2,1,0:T(4,128)S(1)}, u32[]{:S(2)}, u32[]{:S(2)}) async-start(f32[4,3,1152]{2,1,0:T(4,128)} %broadcast_in_dim.29), calls=%async_computation.1 | async-start | bytes 147456 | tf_op jit(solution)/shard_map/all_to_all | solution.py:60
Sparse Core Ops, SparseCore 0:
  11.7 224.5 all-gather.7
  331.5 26.2 reduce-scatter.3
  360.1 79.7 all-reduce.3
  441.8 43.4 all-gather.5
where the time goes:
time: 513 us; the launch traced here: 512 us
  waiting for transfers between devices  318 us (62%)
  blocking collectives  109 us (21%)
  local copies, waits for them, and re-layouts  50.2 us (10%)
  between operations  15.9 us (3%)
  matrix products  11.7 us (2%)
    all_gather x1, waiting for transfers between devices, on_device(): lax.all_gather(w_local, BLK, axis=1, tiled=True)  225 us
    all_gather x5, blocking collectives, gather_in_order(): parts = lax.all_gather(parts, axes[k], axis=0, tiled=True)  81.9 us
    unnamed x5, waiting for transfers between devices  47.5 us
    reduce_scatter x1, waiting for transfers between devices, reduced_to_own(): parts = lax.psum_scatter(parts, axes[k], scatter_dimension=0, tiled=True)  26.4 us
    unnamed x13, local copies, waits for them, and re-layouts  22.7 us
    unnamed x1, blocking collectives  21.6 us
    all_gather x1, waiting for transfers between devices, gather_in_order(): parts = lax.all_gather(parts, axes[k], axis=0, tiled=True)  18.4 us
  transfers between devices with their start and end apart: 5, of which 4 were waited for; matrix products, arithmetic and copies ran while one was open for 5% of the time, Pallas kernels for 0%

commit v1 on v0

--- a/solution.py
+++ b/solution.py
@@ -92,7 +92,11 @@
     live = jnp.where(is_text, 0.0, 1.0).astype(jnp.float32)
     w_local = jnp.where(is_text, caption_reduction_matrix, picture_reduction_matrix)
     outs = jnp.dot(
-        hidden, lax.all_gather(w_local, BLK, axis=1, tiled=True), preferred_element_type=jnp.float32
+        hidden,
+        jnp.concatenate(
+            lax.all_to_all(jnp.stack([w_local] * lax.axis_size(BLK)), BLK, 0, 0), axis=1
+        ),
+        preferred_element_type=jnp.float32,
     )
     text_pool = jnp.mean(outs.reshape(txt_count, TXT_LEN, D), axis=1) + caption_offset_vector
     image_pool = jnp.mean(outs.reshape(img_count, IMG_TOK, D), axis=1) + picture_offset_vector

time: 513 us -> 908 us (1.77)
  waiting for transfers between devices: 318 us -> 615 us
  blocking collectives: 109 us -> 180 us
  starting transfers between devices: 3.41 us -> 23.9 us
    all_to_all x0 -> x1, waiting for transfers between devices: none -> 519 us  [on_device(): lax.all_to_all(jnp.stack([w_local] * lax.axis_size(BLK)), BLK, 0, 0)]
    all_gather x1 -> x0, waiting for transfers between devices: 225 us -> none  [on_device(): lax.all_gather(w_local, BLK, axis=1, tiled=True)]
    all_gather x5, blocking collectives: 81.9 us -> 153 us  [gather_in_order(): parts = lax.all_gather(parts, axes[k], axis=0, tiled=True)]
    all_to_all x0 -> x1, starting transfers between devices: none -> 20.3 us  [on_device(): lax.all_to_all(jnp.stack([w_local] * lax.axis_size(BLK)), BLK, 0, 0)]
    reshape x0 -> x1, local copies, waits for them, and re-layouts: none -> 17.9 us  [on_device(): jnp.concatenate(lax.all_to_all(jnp.stack([w_local] * lax.axis_size(BLK)),...]
    unnamed x13 -> x12, local copies, waits for them, and re-layouts: 22.7 us -> 4.85 us
    unnamed x5 -> x4, waiting for transfers between devices: 47.5 us -> 47.5 us
  transfers between devices with their start and end apart: 5 -> 5, of which waited for: 4 -> 4; matrix products, arithmetic and copies ran while one was open for 5% -> 3% of each run, Pallas kernels for 0% -> 0%
where the time goes in v1:
time: 908 us; the launch traced here: 907 us
  waiting for transfers between devices  615 us (68%)
  blocking collectives  180 us (20%)
  local copies, waits for them, and re-layouts  56.5 us (6%)
  starting transfers between devices  23.9 us (3%)
  between operations  15.9 us (2%)
  matrix products  11.7 us (1%)
    all_to_all x1, waiting for transfers between devices, on_device(): lax.all_to_all(jnp.stack([w_local] * lax.axis_size(BLK)), BLK, 0, 0)  519 us
    all_gather x5, blocking collectives, gather_in_order(): parts = lax.all_gather(parts, axes[k], axis=0, tiled=True)  153 us
    unnamed x4, waiting for transfers between devices  47.5 us
    reduce_scatter x1, waiting for transfers between devices, reduced_to_own(): parts = lax.psum_scatter(parts, axes[k], scatter_dimension=0, tiled=True)  31 us
    unnamed x1, blocking collectives  21.6 us
    all_to_all x1, starting transfers between devices, on_device(): lax.all_to_all(jnp.stack([w_local] * lax.axis_size(BLK)), BLK, 0, 0)  20.3 us
    all_gather x1, waiting for transfers between devices, gather_in_order(): parts = lax.all_gather(parts, axes[k], axis=0, tiled=True)  18.4 us
  transfers between devices with their start and end apart: 5, of which 4 were waited for; matrix products, arithmetic and copies ran while one was open for 3% of the time, Pallas kernels for 0%

profile of v1, /device:TPU:2, one launch (start us, length us, event | category | flops | bytes accessed | tf_op | source)
XLA Modules:
  0.0 907.0 jit_solution(3853355753770131349)
XLA Ops:
  6.5 0.0 copy-start
  6.5 1.1 broadcast_select_fusion
  7.6 6.4 stack.2
  14.0 20.3 %all-to-all-start = ((bf16[128,4304,9]{1,2,0:T(8,128)(2,1)}), bf16[128,4304,9]{1,2,0:T(8,128)(2,1)}, u32[]{:S(2)}, u32[]{:S(2)}) async-start(bf16[128,4304,9]{1,2,0:T(8,128)(2,1)} %stack.2), calls=%async_computation | async-start | bytes 35651584 | tf_op jit(solution)/shard_map/all_to_all | solution.py:97
  34.3 0.0 reduce-scatter.4.cloned.1.call-start
  35.6 1.3 dynamic_slice.10
  36.9 518.5 %all-to-all-done = bf16[128,4304,9]{1,2,0:T(8,128)(2,1)} async-done(((bf16[128,4304,9]{1,2,0:T(8,128)(2,1)}), bf16[128,4304,9]{1,2,0:T(8,128)(2,1)}, u32[]{:S(2)}, u32[]{:S(2)}) %all-to-all-start) | async-done | bytes 9916448 | tf_op jit(solution)/shard_map/all_to_all | solution.py:97
  555.4 17.9 %reshape.151 = bf16[4304,1152]{0,1:T(8,128)(2,1)} reshape(bf16[4304,128,9]{0,2,1:T(8,128)(2,1)} %bitcast.2) | data formatting | bytes 19832832 | tf_op jit(solution)/shard_map/reshape | solution.py:96
  573.3 0.0 copy-done
  573.3 0.0 copy-start.2
  573.3 7.3 fusion.14
  580.5 0.1 reduce_sum.56
  580.6 0.0 copy-done.2
  580.6 5.3 all_gather.22
  585.9 0.1 fusion.4
  586.0 0.1 multiply_convert_fusion
  586.1 44.0 %all_gather.23 = bf16[4,3,1152]{2,1,0:T(4,128)(2,1)S(1)} all-gather(bf16[1,3,1152]{2,1,0:T(4,128)(2,1)S(1)} %multiply_convert_fusion), channel_id=1, replica_groups=mesh['sect'=4,'blk_0'=4,'blk_1'=4,'blk_2'=8] {'blk_0'}, dimensions={0}, use_global_device_ids=true | all-gather | bytes 34560 | tf_op jit(solution)/shard_map/all_gather | solution.py:28
  630.1 10.8 %all_gather.24 = bf16[16,3,1152]{2,1,0:T(4,128)(2,1)S(1)} all-gather(bf16[4,3,1152]{2,1,0:T(4,128)(2,1)S(1)} %all_gather.23), channel_id=1, replica_groups=mesh['sect'=4,'blk_0'=4,'blk_1'=4,'blk_2'=8] {'blk_1'}, dimensions={0}, use_global_device_ids=true | all-gather | bytes 138240 | tf_op jit(solution)/shard_map/all_gather | solution.py:28
  640.9 68.5 %all_gather.25 = bf16[128,3,1152]{2,0,1:T(8,128)(2,1)S(1)} all-gather(bf16[16,3,1152]{2,0,1:T(8,128)(2,1)S(1)} %copy.35), channel_id=1, replica_groups=mesh['sect'=4,'blk_0'=4,'blk_1'=4,'blk_2'=8] {'blk_2'}, dimensions={0}, use_global_device_ids=true | all-gather | bytes 995328 | tf_op jit(solution)/shard_map/all_gather | solution.py:28
  709.4 0.0 copy-start.1
  709.4 1.1 reshape.153
  710.5 1.9 copy.36
  712.5 1.5 reshape_reshape.4
  714.0 0.0 copy-done.1
  714.0 0.6 multiply_reduce_fusion
  715.3 1.5 convolution_reduce_fusion
  716.9 0.6 fusion.12
  717.5 0.2 reshape.159
  717.7 0.9 copy.37
  718.6 1.1 multiply_bitcast_fusion
  719.7 1.8 reshape.155
  721.5 0.0 reduce-scatter.4.cloned.1.call-update
  721.6 0.0 all-reduce.4.cloned.1.call-start
  721.6 31.0 %reduce-scatter.4.cloned.1.call-done = f32[32,3,1152]{2,0,1:T(8,128)} async-done(((f32[128,3,1152]{2,0,1:T(8,128)}), f32[32,3,1152]{2,0,1:T(8,128)}) %reduce-scatter.4.cloned.1.call-update) | async-done | bytes 442384 | tf_op jit(solution)/shard_map/reduce_scatter | solution.py:44
  752.6 0.0 all-reduce.4.cloned.1.call-update
  752.6 0.0 all-gather.4.cloned.1.call-start
  752.6 0.9 dynamic-slice_bitcast_fusion
  753.5 16.7 %all-gather.1 = bf16[4,1076,9]{1,2,0:T(8,128)(2,1)S(1)} all-gather(bf16[1,1076,9]{1,2,0:T(8,128)(2,1)S(1)} %dynamic-slice_bitcast_fusion), channel_id=2, replica_groups=mesh['sect'=4,'blk_0'=4,'blk_1'=4,'blk_2'=8] {'blk_0'}, dimensions={0}, use_global_device_ids=true | all-gather | bytes 96840 | tf_op jit(solution)/shard_map/all_gather | solution.py:28
  770.2 13.0 %all_gather.27 = bf16[16,1076,9]{1,2,0:T(8,128)(2,1)S(1)} all-gather(bf16[4,1076,9]{1,2,0:T(8,128)(2,1)S(1)} %all-gather.1), channel_id=1, replica_groups=mesh['sect'=4,'blk_0'=4,'blk_1'=4,'blk_2'=8] {'blk_1'}, dimensions={0}, use_global_device_ids=true | all-gather | bytes 387360 | tf_op jit(solution)/shard_map/all_gather | solution.py:28
  783.2 0.8 copy.39
  784.0 0.0 all-gather.4.cloned.1.call-update
  784.1 1.3 dynamic-slice
  785.3 1.2 dynamic-slice.2
  787.2 47.4 %all-reduce.4.cloned.1.call-done = f32[32,3,1152]{2,0,1:T(8,128)} async-done(((f32[32,3,1152]{2,0,1:T(8,128)}), f32[32,3,1152]{2,0,1:T(8,128)}) %all-reduce.4.cloned.1.call-update) | async-done | bytes 442384
  834.6 0.9 constant_dynamic-slice_fusion.1
  835.6 21.6 %all-reduce.1 = f32[4,3,1152]{2,0,1:T(4,128)S(1)} all-reduce(f32[4,3,1152]{2,0,1:T(4,128)S(1)} %constant_dynamic-slice_fusion.1), channel_id=5, replica_groups=mesh['sect'=4,'blk_0'=4,'blk_1'=4,'blk_2'=8] {'blk_0'}, use_global_device_ids=true, to_apply=%region_6.7.clone | all-reduce | flops 13824 | bytes 110592
  857.1 0.6 constant_dynamic-slice_fusion
  857.7 0.6 broadcast_in_dim.29
  858.4 3.5 all-to-all-start.1
  861.8 18.4 %all-gather.4.cloned.1.call-done = bf16[128,1076,9]{1,0,2:T(8,128)(2,1)} async-done(((bf16[16,1076,9]{1,0,2:T(8,128)(2,1)}), bf16[128,1076,9]{1,0,2:T(8,128)(2,1)}) %all-gather.4.cloned.1.call-update) | async-done | bytes 2479120 | tf_op jit(solution)/shard_map/all_gather | solution.py:28
  880.2 5.6 reshape.156
  885.8 5.6 copy.42
  891.4 5.9 reshape.158
  897.3 0.0 all-to-all-done.1
  897.4 0.2 fusion.6
  897.6 2.9 fusion.7
  (7 shorter events, 0.1 us)
Async XLA Ops:
  6.5 566.8 %copy-start = (bf16[1,192,4304]{2,1,0:T(8,128)(2,1)S(1)}, bf16[1,192,4304]{2,1,0:T(8,128)(2,1)}, u32[]{:S(2)}) copy-start(bf16[1,192,4304]{2,1,0:T(8,128)(2,1)} %param.8) | copy-start | bytes 4958212
  14.0 541.5 %all-to-all-start = ((bf16[128,4304,9]{1,2,0:T(8,128)(2,1)}), bf16[128,4304,9]{1,2,0:T(8,128)(2,1)}, u32[]{:S(2)}, u32[]{:S(2)}) async-start(bf16[128,4304,9]{1,2,0:T(8,128)(2,1)} %stack.2), calls=%async_computation | async-start | bytes 35651584 | tf_op jit(solution)/shard_map/all_to_all | solution.py:97
  34.3 718.3 %reduce-scatter.4.cloned.1.call-start = ((), (), s32[]{:S(2)}) async-start(), calls=%async_computation.3 | async-start | bytes 2211840 | tf_op jit(solution)/shard_map/reduce_scatter | solution.py:44
  573.3 7.3 copy-start.2
  709.4 4.6 copy-start.1
  721.6 113.1 %all-reduce.4.cloned.1.call-start = ((), (), s32[]{:S(2)}) async-start(), calls=%async_computation.5 | async-start | bytes 884736
  752.6 127.6 %all-gather.4.cloned.1.call-start = ((), (), s32[]{:S(2)}) async-start(), calls=%async_computation.4 | async-start | bytes 2985984 | tf_op jit(solution)/shard_map/all_gather | solution.py:28
  858.4 39.0 %all-to-all-start.1 = ((f32[4,3,1152]{2,1,0:T(4,128)}), f32[4,3,1152]{2,1,0:T(4,128)S(1)}, u32[]{:S(2)}, u32[]{:S(2)}) async-start(f32[4,3,1152]{2,1,0:T(4,128)} %broadcast_in_dim.29), calls=%async_computation.2 | async-start | bytes 147456 | tf_op jit(solution)/shard_map/all_to_all | solution.py:60
Sparse Core Ops, SparseCore 0:
  721.7 30.8 reduce-scatter.3
  754.9 79.7 all-reduce.3
  836.7 43.4 all-gather.3
